TPU v7x, 128 devices: a whole 4x4x4 slice. The times are simulated.
128 devices in a mesh: seq: 16 (over x_lo, y, core), heads: 8 (over z, x_hi).
Axes of the slice: x: 4 (x_hi: 2, x_lo: 2; x = x_hi * 2 + x_lo), y: 4, z: 4, core: 2. Of those that a mesh axis runs over, the one named last changes fastest.
Arguments:
- hidden_in: bfloat16 [4096, 8192], P('seq', 'heads'), may hold values from -6 to 6
- queries: bfloat16 [4096, 8192], P('seq', 'heads'), as said below
- image_kv: bfloat16 [16, 2, 6528, 1024], P('seq', None, None, 'heads'), as said below
- out_weight: bfloat16 [8192, 8192], P('seq', 'heads'), may hold values from -0.0625 to 0.0625
- gate: float32 [1], replicated, may hold values from 0.4 to 1.2
- tile_counts: int32 [16], replicated, may hold values from 1 to 4, as said below
- owners: int32 [256], replicated, may hold values from 0 to 15, as said below
- starts: int32 [256], replicated, may hold values from 0 to 3, as said below
- norm_gain: float32 [8192], P('heads'), may hold values from 0.1 to 1.9
- norm_grad: bfloat16 [4096, 8192], P('seq', 'heads'), may hold values from -6 to 6
- stream_grad: bfloat16 [4096, 8192], P('seq', 'heads'), may hold values from -6 to 6
Outputs:
- hidden_out: bfloat16 [4096, 8192], P('seq', 'heads')
- stream_in_grad: float32 [4096, 8192], P('seq', 'heads')
Inputs may be any that keep to these rules, and one draw needn't show every extreme that they name: `tile_counts`: tiles of each image; some image has 4 tiles in every draw. `owners`: the image (named by the seq index that owns it) that a block of 16 text rows attends to; of the 16 blocks of one seq index at most 2 name the same image, and in every draw some image is named by exactly 2 blocks of every seq index. `starts`: the first tile a block sees, below the tile count of the block's image; in every draw some block starts at tile 0 and some at tile 4 - 1. `image_kv`: keys and values are real-valued. real-valued queries.
All inputs are finite; a program needn't handle non-finite values.
Results may differ from a plain program's by a relative error of at most 0.007.
Values may be sent and summed in bfloat16 or wider, within the bound.
No kernel may reach another device: no remote copies, remote signals or barrier semaphores. Data moves between devices by JAX's collectives and lax.ppermute only.
A program may use at most 128 MiB of HBM per device.

v0:
```python
import math
import jax
import jax.numpy as jnp
from jax import lax
from jax.sharding import PartitionSpec as P

D = 8192
HEAD_DIM = 128
TILE_TOK = 1601
BLOCKS_DEV = 16
CAP = 2
BLK = 16
EPS = 1e-05


def head_scores(query_head, key_block, scale):
    return (
        lax.dot_general(
            query_head, key_block, (((1,), (1,)), ((), ())), preferred_element_type=jnp.float32
        )
        * scale
    )


def local(
    hidden_in,
    queries,
    image_kv,
    out_weight,
    gate,
    tile_counts,
    owners,
    starts,
    norm_gain,
    norm_grad,
    stream_grad,
):
    seq_count = lax.axis_size("seq")
    here = lax.axis_index("seq")
    tok_rows, q_width = queries.shape
    q_heads = q_width // HEAD_DIM
    slot_count = seq_count * CAP
    scale = 1.0 / math.sqrt(HEAD_DIM)
    owner_table = owners.reshape(seq_count, BLOCKS_DEV)
    start_table = starts.reshape(seq_count, BLOCKS_DEV)
    my_owner = lax.dynamic_index_in_dim(owner_table, here, 0, keepdims=False)
    block_ids = jnp.arange(BLOCKS_DEV)
    same = my_owner[:, None] == my_owner[None, :]
    earlier = block_ids[None, :] < block_ids[:, None]
    my_rank = jnp.sum(jnp.logical_and(same, earlier).astype(jnp.int32), axis=1)
    my_slot = my_owner * CAP + my_rank
    placing = (my_slot[:, None] == jnp.arange(slot_count)[None, :]).astype(jnp.bfloat16)
    q_blocks = queries.reshape(BLOCKS_DEV, BLK, q_width)
    outgoing = jnp.einsum(
        "bs,brc->src", placing, q_blocks, preferred_element_type=jnp.float32
    ).astype(jnp.bfloat16)
    outgoing = outgoing.reshape(seq_count, CAP, BLK, q_width)
    arriving = owner_table == here
    arrive_rank = jnp.cumsum(arriving.astype(jnp.int32), axis=1) - 1
    slot_hit = jnp.logical_and(
        arriving[:, :, None], arrive_rank[:, :, None] == jnp.arange(CAP)[None, None, :]
    )
    slot_start = jnp.sum(jnp.where(slot_hit, start_table[:, :, None], 0), axis=1)
    tile_here = lax.dynamic_index_in_dim(tile_counts, here, 0, keepdims=False)
    key_end = tile_here * TILE_TOK
    keys_here = image_kv[0, 0]
    values_here = image_kv[0, 1]
    received = lax.all_to_all(outgoing, "seq", split_axis=0, concat_axis=0, tiled=True)
    flat = received.reshape(-1, q_width)
    row_first = jnp.broadcast_to(slot_start[:, :, None], received.shape[:3]).reshape(-1) * TILE_TOK

    def one_head(head):
        query_head = lax.dynamic_slice_in_dim(flat, head * HEAD_DIM, HEAD_DIM, 1)
        spot = jnp.arange(keys_here.shape[0])
        seen = jnp.logical_and(spot[None, :] >= row_first[:, None], spot[None, :] < key_end)
        scores = jnp.where(seen, head_scores(query_head, keys_here, scale), -jnp.inf)
        highest = jnp.max(scores, axis=1, keepdims=True)
        probs = jnp.exp(scores - highest)
        total = jnp.sum(probs, axis=1, keepdims=True)
        mixed = jnp.dot(probs.astype(jnp.bfloat16), values_here, preferred_element_type=jnp.float32)
        return (mixed / total).astype(jnp.bfloat16)

    heads_out = lax.map(one_head, jnp.arange(q_heads))
    merged = jnp.moveaxis(heads_out, 0, 1).reshape(received.shape)
    returned = lax.all_to_all(merged, "seq", split_axis=0, concat_axis=0, tiled=True)
    context = jnp.einsum(
        "bs,src->brc",
        placing,
        returned.reshape(slot_count, BLK, q_width),
        preferred_element_type=jnp.float32,
    )
    context = context.astype(jnp.bfloat16).reshape(tok_rows, q_width)
    full_context = lax.all_gather(context, "heads", axis=1, tiled=True)
    branch = jnp.dot(
        full_context,
        lax.all_gather(out_weight, "seq", axis=0, tiled=True),
        preferred_element_type=jnp.float32,
    )
    hidden_out = (hidden_in.astype(jnp.float32) + jnp.tanh(gate[0]) * branch).astype(jnp.bfloat16)
    hidden = hidden_out.astype(jnp.float32)
    scaled = norm_gain[None, :] * norm_grad.astype(jnp.float32)
    squares, product = lax.psum(
        (jnp.sum(hidden * hidden, axis=1), jnp.sum(hidden * scaled, axis=1)), "heads"
    )
    inverse = lax.rsqrt(squares / D + EPS)[:, None]
    project = (product / D)[:, None]
    stream_in_grad = (
        stream_grad.astype(jnp.float32) + inverse * scaled - inverse**3 * project * hidden
    )
    return (hidden_out, stream_in_grad)


def solution(mesh):
    placed = (
        P("seq", "heads"),
        P("seq", "heads"),
        P("seq", None, None, "heads"),
        P("seq", "heads"),
        P(),
        P(),
        P(),
        P(),
        P("heads"),
        P("seq", "heads"),
        P("seq", "heads"),
    )
    return jax.shard_map(
        local,
        mesh=mesh,
        in_specs=placed,
        out_specs=(P("seq", "heads"), P("seq", "heads")),
        check_vma=False,
    )
```

profile of v0, /device:TPU:0, one launch (start us, length us, event | category | flops | bytes accessed | tf_op | source)
XLA Modules:
  0.0 361.5 jit_solution(7062695272086445816)
XLA Ops:
  11.2 5.7 %all-to-all-start = ((bf16[16,2,16,1024]{3,1,2,0:T(2,128)(2,1)}), bf16[16,2,16,1024]{3,1,2,0:T(2,128)(2,1)}, u32[]{:S(2)}, u32[]{:S(2)}) async-start(bf16[16,2,16,1024]{3,1,2,0:T(2,128)(2,1)} %copy.36), calls=%async_computation | async-start | bytes 2097152 | tf_op jit(solution)/shard_map/all_to_all | solution.py:68
  18.6 3.4 slice_bitcast_fusion
  21.9 11.6 %all-to-all-done = bf16[16,2,16,1024]{3,1,2,0:T(2,128)(2,1)} async-done(((bf16[16,2,16,1024]{3,1,2,0:T(2,128)(2,1)}), bf16[16,2,16,1024]{3,1,2,0:T(2,128)(2,1)}, u32[]{:S(2)}, u32[]{:S(2)}) %all-to-all-start) | async-done | bytes 1048608 | tf_op jit(solution)/shard_map/all_to_all | solution.py:68
  36.0 95.0 %while.11 = (s32[]{:T(128)}, bf16[8,512,128]{2,1,0:T(8,128)(2,1)}, s32[]{:T(128)}, s32[8]{0:T(128)S(1)}, bf16[512,1024]{1,0:T(8,128)(2,1)}, /*index=5*/bf16[6528...) while((s32[]{:T(128)}, bf16[8,512,128]{2,1,0:T(8,128)(2,1)}, ...), condition=%wide.region_6.7_spmd.clone, body=%wide.region_3.6_spmd.clone.sunk | while | flops 1741493632 | bytes 43744824 | solution.py:83
  37.5 5.6 %fusion.52 = (f32[512]{0:T(512)S(1)}, f32[512,6528]{1,0:T(8,128)S(1)}) fusion(bf16[6528,128]{1,0:T(8,128)(2,1)} %get-tuple-element.183, bf16[512,1024]{1,0:T(8,128)(2,1)} %get-tuple-element.182, s32[]{:T(128)S(6)} %select_n.24, pred[6528]{0:T(1024)(128)(4,1)S(1)} %iota_compare_fusion.6, s32[512]{0:T(512)S(1)} %mul.129), kind=kOutput, calls=%fused_computation.51.clone.1 | convolution fusion | flops 872349184 | bytes 15182212 | tf_op jit(solution)/shard_map/while/body/eval_jaxpr/dot_general | solution.py:18
  45.2 2.7 fusion.54
  49.3 5.6 %fusion.52 = (f32[512]{0:T(512)S(1)}, f32[512,6528]{1,0:T(8,128)S(1)}) fusion(bf16[6528,128]{1,0:T(8,128)(2,1)} %get-tuple-element.183, bf16[512,1024]{1,0:T(8,128)(2,1)} %get-tuple-element.182, s32[]{:T(128)S(6)} %select_n.24, pred[6528]{0:T(1024)(128)(4,1)S(1)} %iota_compare_fusion.6, s32[512]{0:T(512)S(1)} %mul.129), kind=kOutput, calls=%fused_computation.51.clone.1 | convolution fusion | flops 872349184 | bytes 15182212 | tf_op jit(solution)/shard_map/while/body/eval_jaxpr/dot_general | solution.py:18
  57.0 2.7 fusion.54
  61.2 5.6 %fusion.52 = (f32[512]{0:T(512)S(1)}, f32[512,6528]{1,0:T(8,128)S(1)}) fusion(bf16[6528,128]{1,0:T(8,128)(2,1)} %get-tuple-element.183, bf16[512,1024]{1,0:T(8,128)(2,1)} %get-tuple-element.182, s32[]{:T(128)S(6)} %select_n.24, pred[6528]{0:T(1024)(128)(4,1)S(1)} %iota_compare_fusion.6, s32[512]{0:T(512)S(1)} %mul.129), kind=kOutput, calls=%fused_computation.51.clone.1 | convolution fusion | flops 872349184 | bytes 15182212 | tf_op jit(solution)/shard_map/while/body/eval_jaxpr/dot_general | solution.py:18
  68.9 2.7 fusion.54
  73.1 5.6 %fusion.52 = (f32[512]{0:T(512)S(1)}, f32[512,6528]{1,0:T(8,128)S(1)}) fusion(bf16[6528,128]{1,0:T(8,128)(2,1)} %get-tuple-element.183, bf16[512,1024]{1,0:T(8,128)(2,1)} %get-tuple-element.182, s32[]{:T(128)S(6)} %select_n.24, pred[6528]{0:T(1024)(128)(4,1)S(1)} %iota_compare_fusion.6, s32[512]{0:T(512)S(1)} %mul.129), kind=kOutput, calls=%fused_computation.51.clone.1 | convolution fusion | flops 872349184 | bytes 15182212 | tf_op jit(solution)/shard_map/while/body/eval_jaxpr/dot_general | solution.py:18
  80.8 2.7 fusion.54
  84.9 5.6 %fusion.52 = (f32[512]{0:T(512)S(1)}, f32[512,6528]{1,0:T(8,128)S(1)}) fusion(bf16[6528,128]{1,0:T(8,128)(2,1)} %get-tuple-element.183, bf16[512,1024]{1,0:T(8,128)(2,1)} %get-tuple-element.182, s32[]{:T(128)S(6)} %select_n.24, pred[6528]{0:T(1024)(128)(4,1)S(1)} %iota_compare_fusion.6, s32[512]{0:T(512)S(1)} %mul.129), kind=kOutput, calls=%fused_computation.51.clone.1 | convolution fusion | flops 872349184 | bytes 15182212 | tf_op jit(solution)/shard_map/while/body/eval_jaxpr/dot_general | solution.py:18
  92.7 2.7 fusion.54
  96.8 5.6 %fusion.52 = (f32[512]{0:T(512)S(1)}, f32[512,6528]{1,0:T(8,128)S(1)}) fusion(bf16[6528,128]{1,0:T(8,128)(2,1)} %get-tuple-element.183, bf16[512,1024]{1,0:T(8,128)(2,1)} %get-tuple-element.182, s32[]{:T(128)S(6)} %select_n.24, pred[6528]{0:T(1024)(128)(4,1)S(1)} %iota_compare_fusion.6, s32[512]{0:T(512)S(1)} %mul.129), kind=kOutput, calls=%fused_computation.51.clone.1 | convolution fusion | flops 872349184 | bytes 15182212 | tf_op jit(solution)/shard_map/while/body/eval_jaxpr/dot_general | solution.py:18
  104.5 2.7 fusion.54
  108.7 5.6 %fusion.52 = (f32[512]{0:T(512)S(1)}, f32[512,6528]{1,0:T(8,128)S(1)}) fusion(bf16[6528,128]{1,0:T(8,128)(2,1)} %get-tuple-element.183, bf16[512,1024]{1,0:T(8,128)(2,1)} %get-tuple-element.182, s32[]{:T(128)S(6)} %select_n.24, pred[6528]{0:T(1024)(128)(4,1)S(1)} %iota_compare_fusion.6, s32[512]{0:T(512)S(1)} %mul.129), kind=kOutput, calls=%fused_computation.51.clone.1 | convolution fusion | flops 872349184 | bytes 15182212 | tf_op jit(solution)/shard_map/while/body/eval_jaxpr/dot_general | solution.py:18
  120.6 5.6 %fusion.52 = (f32[512]{0:T(512)S(1)}, f32[512,6528]{1,0:T(8,128)S(1)}) fusion(bf16[6528,128]{1,0:T(8,128)(2,1)} %get-tuple-element.183, bf16[512,1024]{1,0:T(8,128)(2,1)} %get-tuple-element.182, s32[]{:T(128)S(6)} %select_n.24, pred[6528]{0:T(1024)(128)(4,1)S(1)} %iota_compare_fusion.6, s32[512]{0:T(512)S(1)} %mul.129), kind=kOutput, calls=%fused_computation.51.clone.1 | convolution fusion | flops 872349184 | bytes 15182212 | tf_op jit(solution)/shard_map/while/body/eval_jaxpr/dot_general | solution.py:18
  128.3 2.7 fusion.54
  133.4 19.1 %all_to_all.10 = bf16[16,2,16,1024]{3,2,1,0:T(8,128)(2,1)S(1)} all-to-all(bf16[16,2,16,1024]{3,2,1,0:T(8,128)(2,1)S(1)} %reshape.80), channel_id=1, replica_groups=mesh['seq'=16,'heads'=8] {'seq'}, dimensions={0} | all-to-all | bytes 2097152 | tf_op jit(solution)/shard_map/all_to_all | solution.py:85
  156.3 69.8 %all-gather.3.cloned.1.call-done = bf16[256,8192]{1,0:T(8,128)(2,1)} async-done(((bf16[256,1024]{1,0:T(8,128)(2,1)}), bf16[256,8192]{1,0:T(8,128)(2,1)}) %all-gather.3.cloned.1.call-update) | async-done | bytes 4194320 | tf_op jit(solution)/shard_map/all_gather | solution.py:93
  226.0 91.0 %all-gather.5.cloned.1.call-done = bf16[8192,1024]{1,0:T(8,128)(2,1)} async-done(((bf16[512,1024]{1,0:T(8,128)(2,1)}), bf16[8192,1024]{1,0:T(8,128)(2,1)}) %all-gather.5.cloned.1.call-update) | async-done | bytes 16777232 | tf_op jit(solution)/shard_map/all_gather | solution.py:96
  317.1 11.8 %fusion.24 = (f32[256]{0:T(256)S(1)}, f32[256]{0:T(256)S(1)}, bf16[256,1024]{1,0:T(8,128)(2,1)S(1)}) fusion(bf16[256,1024]{1,0:T(8,128)(2,1)S(1)} %copy-done.1, f32[1024]{0:T(1024)S(1)} %copy-done.4, bf16[256,8192]{1,0:T(8,128)(2,1)} %all-gather.3.cloned.1.call-done, bf16[8192,1024]{1,0:T(8,128)(2,1)} %all-gather.5.cloned.1.call-done, f32[]{:T(128)} %bitcast, ...), kind=kOutput, calls=%fused_computation.26 | convolution fusion | flops 4297850880 | bytes 22550532 | tf_op jit(solution)/shard_map/dot_general | solution.py:94
  328.9 24.4 %all-reduce = (f32[256]{0:T(256)S(1)}, f32[256]{0:T(256)S(1)}) all-reduce(f32[256]{0:T(256)S(1)} %get-tuple-element.73, f32[256]{0:T(256)S(1)} %get-tuple-element.72), channel_id=1, replica_groups=mesh['seq'=16,'heads'=8] {'heads'}, use_global_device_ids=true, to_apply=%region_10.11 | all-reduce | flops 512 | bytes 4096 | tf_op jit(solution)/shard_map/psum | solution.py:102
  (83 shorter events, 40.5 us)
Async XLA Ops:
  7.2 1.1 copy-start
  7.2 10.0 %copy-start.5 = (s32[256]{0:T(256)S(1)}, s32[256]{0:T(256)}, u32[]{:S(2)}) copy-start(s32[256]{0:T(256)} %param.20) | copy-start | bytes 3076
  7.2 10.3 %copy-start.6 = (s32[16]{0:T(128)S(1)}, s32[16]{0:T(128)}, u32[]{:S(2)}) copy-start(s32[16]{0:T(128)} %param.18) | copy-start | bytes 196
  11.2 22.3 %all-to-all-start = ((bf16[16,2,16,1024]{3,1,2,0:T(2,128)(2,1)}), bf16[16,2,16,1024]{3,1,2,0:T(2,128)(2,1)}, u32[]{:S(2)}, u32[]{:S(2)}) async-start(bf16[16,2,16,1024]{3,1,2,0:T(2,128)(2,1)} %copy.36), calls=%async_computation | async-start | bytes 2097152 | tf_op jit(solution)/shard_map/all_to_all | solution.py:68
  16.9 209.1 %all-gather.3.cloned.1.call-start = ((), (), s32[]{:S(2)}) async-start(), calls=%async_computation.2 | async-start | bytes 4718592 | tf_op jit(solution)/shard_map/all_gather | solution.py:93
  131.0 186.1 %copy-start.1 = (bf16[256,1024]{1,0:T(8,128)(2,1)S(1)}, bf16[256,1024]{1,0:T(8,128)(2,1)}, u32[]{:S(2)}) copy-start(bf16[256,1024]{1,0:T(8,128)(2,1)} %param.22) | copy-start | bytes 1572868
  131.0 186.1 %copy-start.4 = (f32[1024]{0:T(1024)S(1)}, f32[1024]{0:T(1024)}, u32[]{:S(2)}) copy-start(f32[1024]{0:T(1024)} %param.21) | copy-start | bytes 12292
  154.8 162.2 %all-gather.5.cloned.1.call-start = ((), (), s32[]{:S(2)}) async-start(), calls=%async_computation.3 | async-start | bytes 17825792 | tf_op jit(solution)/shard_map/all_gather | solution.py:96
  317.1 36.3 %copy-start.2 = (bf16[256,1024]{1,0:T(8,128)(2,1)S(1)}, bf16[256,1024]{1,0:T(8,128)(2,1)}, u32[]{:S(2)}) copy-start(bf16[256,1024]{1,0:T(8,128)(2,1)} %param.23) | copy-start | bytes 1572868
  328.9 25.7 %copy-start.3 = (bf16[256,1024]{1,0:T(8,128)(2,1)}, bf16[256,1024]{1,0:T(8,128)(2,1)S(1)}, u32[]{:S(2)}) copy-start(bf16[256,1024]{1,0:T(8,128)(2,1)S(1)} %get-tuple-element.100) | copy-start | bytes 1572868
Sparse Core Ops, SparseCore 0:
  155.0 71.0 all-gather.2
  227.8 89.2 all-gather.4
where the time goes:
time: 362 us; the launch traced here: 361 us
  waiting for transfers between devices  173 us (48%)
  matrix products  80 us (22%)
  blocking collectives  43.5 us (12%)
  local copies, waits for them, and re-layouts  19.9 us (5%)
  other arithmetic  18.7 us (5%)
  between operations  15.4 us (4%)
  starting transfers between devices  5.93 us (2%)
  loops' own time  5.21 us (1%)
    all_gather x1, waiting for transfers between devices, local(): lax.all_gather(out_weight, 'seq', axis=0, tiled=True)  91 us
    all_gather x1, waiting for transfers between devices, local(): full_context = lax.all_gather(context, 'heads', axis=1, tiled=True)  69.8 us
    dot_general x8, matrix products, head_scores(): lax.dot_general(query_head, key_block, (((1,), (1,)), ((), ())), preferre...  44.9 us
    psum x1, blocking collectives, local(): lax.psum((jnp.sum(hidden * hidden, axis=1), jnp.sum(hidden * scaled, axis...  24.4 us
    dot_general x8, matrix products, one_head(): jnp.dot(probs.astype(jnp.bfloat16), values_here, preferred_element_type=j...  21.5 us
    all_to_all x1, blocking collectives, local(): lax.all_to_all(merged, 'seq', split_axis=0, concat_axis=0, tiled=True)  19.1 us
    reduce_sum x8, other arithmetic, one_head(): total = jnp.sum(probs, axis=1, keepdims=True)  16.8 us
    dot_general x1, matrix products, local(): jnp.dot(full_context, lax.all_gather(out_weight, 'seq', axis=0, tiled=Tru...  11.8 us
  transfers between devices with their start and end apart: 3, of which 3 were waited for; matrix products, arithmetic and copies ran while one was open for 1% of the time, Pallas kernels for 0%

commit v1 on v0

--- a/solution.py
+++ b/solution.py
@@ -90,7 +90,10 @@
         preferred_element_type=jnp.float32,
     )
     context = context.astype(jnp.bfloat16).reshape(tok_rows, q_width)
-    full_context = lax.all_gather(context, "heads", axis=1, tiled=True)
+    response = jax.lax.psum(1, "heads")
+    seen_now = jnp.stack(response * [context])
+    inter = jax.lax.all_to_all(seen_now, "heads", 0, 0)
+    full_context = jnp.concatenate(inter, axis=1)
     branch = jnp.dot(
         full_context,
         lax.all_gather(out_weight, "seq", axis=0, tiled=True),

time: 362 us -> 267 us (0.74)
  waiting for transfers between devices: 173 us -> 71.1 us
  starting transfers between devices: 5.93 us -> 14.3 us
  blocking collectives: 43.5 us -> 39.5 us
    all_gather x1, waiting for transfers between devices: 91 us -> 0.01 us  [local(): lax.all_gather(out_weight, 'seq', axis=0, tiled=True)]
    all_gather x1 -> x0, waiting for transfers between devices: 69.8 us -> none  [local(): full_context = lax.all_gather(context, 'heads', axis=1, tiled=True)]
    all_to_all x0 -> x1, waiting for transfers between devices: none -> 49.8 us  [local(): inter = jax.lax.all_to_all(seen_now, 'heads', 0, 0)]
    all_to_all x1, waiting for transfers between devices: 11.6 us -> 20.6 us  [local(): lax.all_to_all(outgoing, 'seq', split_axis=0, concat_axis=0, tiled=True)]
    all_to_all x0 -> x1, starting transfers between devices: none -> 8.63 us  [local(): inter = jax.lax.all_to_all(seen_now, 'heads', 0, 0)]
    psum x1, blocking collectives: 24.4 us -> 20.5 us  [local(): lax.psum((jnp.sum(hidden * hidden, axis=1), jnp.sum(hidden * scaled, axis...]
  transfers between devices with their start and end apart: 3 -> 3, of which waited for: 3 -> 2; matrix products, arithmetic and copies ran while one was open for 1% -> 40% of each run, Pallas kernels for 0% -> 0%
where the time goes in v1:
time: 267 us
  matrix products  80.2 us (30%)
  waiting for transfers between devices  71.1 us (27%)
  blocking collectives  39.5 us (15%)
  local copies, waits for them, and re-layouts  21.7 us (8%)
  other arithmetic  18.7 us (7%)
  between operations  15.5 us (6%)
  starting transfers between devices  14.3 us (5%)
  loops' own time  5.68 us (2%)
    all_to_all x1, waiting for transfers between devices, local(): inter = jax.lax.all_to_all(seen_now, 'heads', 0, 0)  49.8 us
    dot_general x8, matrix products, head_scores(): lax.dot_general(query_head, key_block, (((1,), (1,)), ((), ())), preferre...  45.1 us
    dot_general x8, matrix products, one_head(): jnp.dot(probs.astype(jnp.bfloat16), values_here, preferred_element_type=j...  21.5 us
    all_to_all x1, waiting for transfers between devices, local(): lax.all_to_all(outgoing, 'seq', split_axis=0, concat_axis=0, tiled=True)  20.6 us
    psum x1, blocking collectives, local(): lax.psum((jnp.sum(hidden * hidden, axis=1), jnp.sum(hidden * scaled, axis...  20.5 us
    all_to_all x1, blocking collectives, local(): lax.all_to_all(merged, 'seq', split_axis=0, concat_axis=0, tiled=True)  19.1 us
    reduce_sum x8, other arithmetic, one_head(): total = jnp.sum(probs, axis=1, keepdims=True)  16.8 us
    dot_general x1, matrix products, local(): jnp.dot(full_context, lax.all_gather(out_weight, 'seq', axis=0, tiled=Tru...  11.9 us
  transfers between devices with their start and end apart: 3, of which 2 were waited for; matrix products, arithmetic and copies ran while one was open for 40% of the time, Pallas kernels for 0%

profile of v1, /device:TPU:0, one launch (start us, length us, event | category | flops | bytes accessed | tf_op | source)
XLA Modules:
  0.0 266.6 jit_solution(3042900136336205248)
XLA Ops:
  11.9 5.7 %all-to-all-start = ((bf16[16,2,16,1024]{3,1,2,0:T(2,128)(2,1)}), bf16[16,2,16,1024]{3,1,2,0:T(2,128)(2,1)}, u32[]{:S(2)}, u32[]{:S(2)}) async-start(bf16[16,2,16,1024]{3,1,2,0:T(2,128)(2,1)} %copy.39), calls=%async_computation | async-start | bytes 2097152 | tf_op jit(solution)/shard_map/all_to_all | solution.py:68
  19.3 3.4 %slice_bitcast_fusion = (bf16[6528,128]{1,0:T(8,128)(2,1)S(1)}, bf16[6528,128]{1,0:T(8,128)(2,1)}) fusion(bf16[1,2,6528,128]{3,2,1,0:T(8,128)(2,1)} %param.15), kind=kLoop, calls=%fused_computation.16 | loop fusion | bytes 6684672 | tf_op jit(solution)/shard_map/squeeze | solution.py:67
  22.6 20.6 %all-to-all-done = bf16[16,2,16,1024]{3,1,2,0:T(2,128)(2,1)} async-done(((bf16[16,2,16,1024]{3,1,2,0:T(2,128)(2,1)}), bf16[16,2,16,1024]{3,1,2,0:T(2,128)(2,1)}, u32[]{:S(2)}, u32[]{:S(2)}) %all-to-all-start) | async-done | bytes 1048608 | tf_op jit(solution)/shard_map/all_to_all | solution.py:68
  45.8 95.8 %while.11 = (s32[]{:T(128)}, bf16[8,512,128]{2,1,0:T(8,128)(2,1)}, s32[]{:T(128)}, s32[8]{0:T(128)S(1)}, bf16[512,1024]{1,0:T(8,128)(2,1)}, /*index=5*/bf16[6528...) while((s32[]{:T(128)}, bf16[8,512,128]{2,1,0:T(8,128)(2,1)}, ...), condition=%wide.region_6.7_spmd.clone, body=%wide.region_3.6_spmd.clone.sunk | while | flops 1741493632 | bytes 43744824 | solution.py:83
  47.3 5.6 %fusion.52 = (f32[512]{0:T(512)S(1)}, f32[512,6528]{1,0:T(8,128)S(1)}) fusion(bf16[6528,128]{1,0:T(8,128)(2,1)} %get-tuple-element.183, bf16[512,1024]{1,0:T(8,128)(2,1)} %get-tuple-element.182, s32[]{:T(128)S(6)} %select_n.24, pred[6528]{0:T(1024)(128)(4,1)S(1)} %iota_compare_fusion.6, s32[512]{0:T(512)S(1)} %mul.129), kind=kOutput, calls=%fused_computation.51.clone.1 | convolution fusion | flops 872349184 | bytes 15182212 | tf_op jit(solution)/shard_map/while/body/eval_jaxpr/dot_general | solution.py:18
  55.1 2.7 %fusion.54 = bf16[8,512,128]{2,1,0:T(8,128)(2,1)} fusion(bf16[8,512,128]{2,1,0:T(8,128)(2,1)} %get-tuple-element.167, s32[]{:T(128)} %get-tuple-element.166, bf16[6528,128]{1,0:T(8,128)(2,1)S(1)} %get-tuple-element.184, f32[512,6528]{1,0:T(8,128)S(1)} %get-tuple-element.152, f32[512]{0:T(512)S(1)} %get-tuple-element.153, f32[512]{0:T(512)S(1)} %fusion.53), kind=kOutput, calls=%fused_computation.12.clone.1 | convolution fusion | flops 862453760 | bytes 15176192 | tf_op jit(solution)/shard_map/while/body/eval_jaxpr/dot_general | solution.py:80
  59.3 5.6 %fusion.52 = (f32[512]{0:T(512)S(1)}, f32[512,6528]{1,0:T(8,128)S(1)}) fusion(bf16[6528,128]{1,0:T(8,128)(2,1)} %get-tuple-element.183, bf16[512,1024]{1,0:T(8,128)(2,1)} %get-tuple-element.182, s32[]{:T(128)S(6)} %select_n.24, pred[6528]{0:T(1024)(128)(4,1)S(1)} %iota_compare_fusion.6, s32[512]{0:T(512)S(1)} %mul.129), kind=kOutput, calls=%fused_computation.51.clone.1 | convolution fusion | flops 872349184 | bytes 15182212 | tf_op jit(solution)/shard_map/while/body/eval_jaxpr/dot_general | solution.py:18
  67.0 2.7 %fusion.54 = bf16[8,512,128]{2,1,0:T(8,128)(2,1)} fusion(bf16[8,512,128]{2,1,0:T(8,128)(2,1)} %get-tuple-element.167, s32[]{:T(128)} %get-tuple-element.166, bf16[6528,128]{1,0:T(8,128)(2,1)S(1)} %get-tuple-element.184, f32[512,6528]{1,0:T(8,128)S(1)} %get-tuple-element.152, f32[512]{0:T(512)S(1)} %get-tuple-element.153, f32[512]{0:T(512)S(1)} %fusion.53), kind=kOutput, calls=%fused_computation.12.clone.1 | convolution fusion | flops 862453760 | bytes 15176192 | tf_op jit(solution)/shard_map/while/body/eval_jaxpr/dot_general | solution.py:80
  71.2 5.7 %fusion.52 = (f32[512]{0:T(512)S(1)}, f32[512,6528]{1,0:T(8,128)S(1)}) fusion(bf16[6528,128]{1,0:T(8,128)(2,1)} %get-tuple-element.183, bf16[512,1024]{1,0:T(8,128)(2,1)} %get-tuple-element.182, s32[]{:T(128)S(6)} %select_n.24, pred[6528]{0:T(1024)(128)(4,1)S(1)} %iota_compare_fusion.6, s32[512]{0:T(512)S(1)} %mul.129), kind=kOutput, calls=%fused_computation.51.clone.1 | convolution fusion | flops 872349184 | bytes 15182212 | tf_op jit(solution)/shard_map/while/body/eval_jaxpr/dot_general | solution.py:18
  79.1 2.7 %fusion.54 = bf16[8,512,128]{2,1,0:T(8,128)(2,1)} fusion(bf16[8,512,128]{2,1,0:T(8,128)(2,1)} %get-tuple-element.167, s32[]{:T(128)} %get-tuple-element.166, bf16[6528,128]{1,0:T(8,128)(2,1)S(1)} %get-tuple-element.184, f32[512,6528]{1,0:T(8,128)S(1)} %get-tuple-element.152, f32[512]{0:T(512)S(1)} %get-tuple-element.153, f32[512]{0:T(512)S(1)} %fusion.53), kind=kOutput, calls=%fused_computation.12.clone.1 | convolution fusion | flops 862453760 | bytes 15176192 | tf_op jit(solution)/shard_map/while/body/eval_jaxpr/dot_general | solution.py:80
  83.3 5.6 %fusion.52 = (f32[512]{0:T(512)S(1)}, f32[512,6528]{1,0:T(8,128)S(1)}) fusion(bf16[6528,128]{1,0:T(8,128)(2,1)} %get-tuple-element.183, bf16[512,1024]{1,0:T(8,128)(2,1)} %get-tuple-element.182, s32[]{:T(128)S(6)} %select_n.24, pred[6528]{0:T(1024)(128)(4,1)S(1)} %iota_compare_fusion.6, s32[512]{0:T(512)S(1)} %mul.129), kind=kOutput, calls=%fused_computation.51.clone.1 | convolution fusion | flops 872349184 | bytes 15182212 | tf_op jit(solution)/shard_map/while/body/eval_jaxpr/dot_general | solution.py:18
  95.3 5.6 %fusion.52 = (f32[512]{0:T(512)S(1)}, f32[512,6528]{1,0:T(8,128)S(1)}) fusion(bf16[6528,128]{1,0:T(8,128)(2,1)} %get-tuple-element.183, bf16[512,1024]{1,0:T(8,128)(2,1)} %get-tuple-element.182, s32[]{:T(128)S(6)} %select_n.24, pred[6528]{0:T(1024)(128)(4,1)S(1)} %iota_compare_fusion.6, s32[512]{0:T(512)S(1)} %mul.129), kind=kOutput, calls=%fused_computation.51.clone.1 | convolution fusion | flops 872349184 | bytes 15182212 | tf_op jit(solution)/shard_map/while/body/eval_jaxpr/dot_general | solution.py:18
  103.0 2.7 %fusion.54 = bf16[8,512,128]{2,1,0:T(8,128)(2,1)} fusion(bf16[8,512,128]{2,1,0:T(8,128)(2,1)} %get-tuple-element.167, s32[]{:T(128)} %get-tuple-element.166, bf16[6528,128]{1,0:T(8,128)(2,1)S(1)} %get-tuple-element.184, f32[512,6528]{1,0:T(8,128)S(1)} %get-tuple-element.152, f32[512]{0:T(512)S(1)} %get-tuple-element.153, f32[512]{0:T(512)S(1)} %fusion.53), kind=kOutput, calls=%fused_computation.12.clone.1 | convolution fusion | flops 862453760 | bytes 15176192 | tf_op jit(solution)/shard_map/while/body/eval_jaxpr/dot_general | solution.py:80
  107.3 5.6 %fusion.52 = (f32[512]{0:T(512)S(1)}, f32[512,6528]{1,0:T(8,128)S(1)}) fusion(bf16[6528,128]{1,0:T(8,128)(2,1)} %get-tuple-element.183, bf16[512,1024]{1,0:T(8,128)(2,1)} %get-tuple-element.182, s32[]{:T(128)S(6)} %select_n.24, pred[6528]{0:T(1024)(128)(4,1)S(1)} %iota_compare_fusion.6, s32[512]{0:T(512)S(1)} %mul.129), kind=kOutput, calls=%fused_computation.51.clone.1 | convolution fusion | flops 872349184 | bytes 15182212 | tf_op jit(solution)/shard_map/while/body/eval_jaxpr/dot_general | solution.py:18
  115.0 2.7 %fusion.54 = bf16[8,512,128]{2,1,0:T(8,128)(2,1)} fusion(bf16[8,512,128]{2,1,0:T(8,128)(2,1)} %get-tuple-element.167, s32[]{:T(128)} %get-tuple-element.166, bf16[6528,128]{1,0:T(8,128)(2,1)S(1)} %get-tuple-element.184, f32[512,6528]{1,0:T(8,128)S(1)} %get-tuple-element.152, f32[512]{0:T(512)S(1)} %get-tuple-element.153, f32[512]{0:T(512)S(1)} %fusion.53), kind=kOutput, calls=%fused_computation.12.clone.1 | convolution fusion | flops 862453760 | bytes 15176192 | tf_op jit(solution)/shard_map/while/body/eval_jaxpr/dot_general | solution.py:80
  119.2 5.6 %fusion.52 = (f32[512]{0:T(512)S(1)}, f32[512,6528]{1,0:T(8,128)S(1)}) fusion(bf16[6528,128]{1,0:T(8,128)(2,1)} %get-tuple-element.183, bf16[512,1024]{1,0:T(8,128)(2,1)} %get-tuple-element.182, s32[]{:T(128)S(6)} %select_n.24, pred[6528]{0:T(1024)(128)(4,1)S(1)} %iota_compare_fusion.6, s32[512]{0:T(512)S(1)} %mul.129), kind=kOutput, calls=%fused_computation.51.clone.1 | convolution fusion | flops 872349184 | bytes 15182212 | tf_op jit(solution)/shard_map/while/body/eval_jaxpr/dot_general | solution.py:18
  126.9 2.7 %fusion.54 = bf16[8,512,128]{2,1,0:T(8,128)(2,1)} fusion(bf16[8,512,128]{2,1,0:T(8,128)(2,1)} %get-tuple-element.167, s32[]{:T(128)} %get-tuple-element.166, bf16[6528,128]{1,0:T(8,128)(2,1)S(1)} %get-tuple-element.184, f32[512,6528]{1,0:T(8,128)S(1)} %get-tuple-element.152, f32[512]{0:T(512)S(1)} %get-tuple-element.153, f32[512]{0:T(512)S(1)} %fusion.53), kind=kOutput, calls=%fused_computation.12.clone.1 | convolution fusion | flops 862453760 | bytes 15176192 | tf_op jit(solution)/shard_map/while/body/eval_jaxpr/dot_general | solution.py:80
  131.2 5.6 %fusion.52 = (f32[512]{0:T(512)S(1)}, f32[512,6528]{1,0:T(8,128)S(1)}) fusion(bf16[6528,128]{1,0:T(8,128)(2,1)} %get-tuple-element.183, bf16[512,1024]{1,0:T(8,128)(2,1)} %get-tuple-element.182, s32[]{:T(128)S(6)} %select_n.24, pred[6528]{0:T(1024)(128)(4,1)S(1)} %iota_compare_fusion.6, s32[512]{0:T(512)S(1)} %mul.129), kind=kOutput, calls=%fused_computation.51.clone.1 | convolution fusion | flops 872349184 | bytes 15182212 | tf_op jit(solution)/shard_map/while/body/eval_jaxpr/dot_general | solution.py:18
  138.9 2.7 %fusion.54 = bf16[8,512,128]{2,1,0:T(8,128)(2,1)} fusion(bf16[8,512,128]{2,1,0:T(8,128)(2,1)} %get-tuple-element.167, s32[]{:T(128)} %get-tuple-element.166, bf16[6528,128]{1,0:T(8,128)(2,1)S(1)} %get-tuple-element.184, f32[512,6528]{1,0:T(8,128)S(1)} %get-tuple-element.152, f32[512]{0:T(512)S(1)} %get-tuple-element.153, f32[512]{0:T(512)S(1)} %fusion.53), kind=kOutput, calls=%fused_computation.12.clone.1 | convolution fusion | flops 862453760 | bytes 15176192 | tf_op jit(solution)/shard_map/while/body/eval_jaxpr/dot_general | solution.py:80
  144.0 19.1 %all_to_all.15 = bf16[16,2,16,1024]{3,2,1,0:T(8,128)(2,1)S(1)} all-to-all(bf16[16,2,16,1024]{3,2,1,0:T(8,128)(2,1)S(1)} %reshape.85), channel_id=1, replica_groups=mesh['seq'=16,'heads'=8] {'seq'}, dimensions={0} | all-to-all | bytes 2097152 | tf_op jit(solution)/shard_map/all_to_all | solution.py:85
  167.0 8.6 %all-to-all-start.2 = ((bf16[8,256,1024]{1,2,0:T(8,128)(2,1)}), bf16[8,256,1024]{1,2,0:T(8,128)(2,1)}, u32[]{:S(2)}, u32[]{:S(2)}) async-start(bf16[8,256,1024]{1,2,0:T(8,128)(2,1)} %stack.3), calls=%async_computation.2 | async-start | bytes 8388608 | tf_op jit(solution)/shard_map/all_to_all | solution.py:95
  176.3 49.8 %all-to-all-done.2 = bf16[8,256,1024]{1,2,0:T(8,128)(2,1)} async-done(((bf16[8,256,1024]{1,2,0:T(8,128)(2,1)}), bf16[8,256,1024]{1,2,0:T(8,128)(2,1)}, u32[]{:S(2)}, u32[]{:S(2)}) %all-to-all-start.2) | async-done | bytes 4194336 | tf_op jit(solution)/shard_map/all_to_all | solution.py:95
  226.2 11.9 %fusion.24 = (f32[256]{0:T(256)S(1)}, f32[256]{0:T(256)S(1)}, bf16[256,1024]{1,0:T(8,128)(2,1)S(1)}) fusion(bf16[256,1024]{1,0:T(8,128)(2,1)S(1)} %copy-done.1, f32[1024]{0:T(1024)S(1)} %copy-done.5, bf16[256,8192]{0,1:T(8,128)(2,1)} %bitcast.12, bf16[8192,1024]{1,0:T(8,128)(2,1)} %all-gather.2.cloned.1.call-done, f32[]{:T(128)} %bitcast, ...), kind=kOutput, calls=%fused_computation.26 | convolution fusion | flops 4297850880 | bytes 22550532 | tf_op jit(solution)/shard_map/dot_general | solution.py:97
  238.0 20.5 %all-reduce = (f32[256]{0:T(256)S(1)}, f32[256]{0:T(256)S(1)}) all-reduce(f32[256]{0:T(256)S(1)} %get-tuple-element.73, f32[256]{0:T(256)S(1)} %get-tuple-element.72), channel_id=1, replica_groups=mesh['seq'=16,'heads'=8] {'heads'}, use_global_device_ids=true, to_apply=%region_10.11 | all-reduce | flops 512 | bytes 4096 | tf_op jit(solution)/shard_map/psum | solution.py:105
  (86 shorter events, 42.2 us)
Async XLA Ops:
  7.2 1.7 copy-start
  7.2 10.6 %copy-start.6 = (s32[256]{0:T(256)S(1)}, s32[256]{0:T(256)}, u32[]{:S(2)}) copy-start(s32[256]{0:T(256)} %param.20) | copy-start | bytes 3076
  7.2 10.9 %copy-start.7 = (s32[16]{0:T(128)S(1)}, s32[16]{0:T(128)}, u32[]{:S(2)}) copy-start(s32[16]{0:T(128)} %param.18) | copy-start | bytes 196
  7.2 218.9 %all-gather.2.cloned.1.call-start = ((), (), s32[]{:S(2)}) async-start(), calls=%async_computation.3 | async-start | bytes 17825792 | tf_op jit(solution)/shard_map/all_gather | solution.py:99
  11.9 31.3 %all-to-all-start = ((bf16[16,2,16,1024]{3,1,2,0:T(2,128)(2,1)}), bf16[16,2,16,1024]{3,1,2,0:T(2,128)(2,1)}, u32[]{:S(2)}, u32[]{:S(2)}) async-start(bf16[16,2,16,1024]{3,1,2,0:T(2,128)(2,1)} %copy.39), calls=%async_computation | async-start | bytes 2097152 | tf_op jit(solution)/shard_map/all_to_all | solution.py:68
  164.8 61.4 %copy-start.1 = (bf16[256,1024]{1,0:T(8,128)(2,1)S(1)}, bf16[256,1024]{1,0:T(8,128)(2,1)}, u32[]{:S(2)}) copy-start(bf16[256,1024]{1,0:T(8,128)(2,1)} %param.22) | copy-start | bytes 1572868
  164.8 61.4 %copy-start.3 = (bf16[256,1024]{1,0:T(8,128)(2,1)S(1)}, bf16[256,1024]{1,0:T(8,128)(2,1)}, u32[]{:S(2)}) copy-start(bf16[256,1024]{1,0:T(8,128)(2,1)} %param.13) | copy-start | bytes 1572868
  164.8 61.4 %copy-start.5 = (f32[1024]{0:T(1024)S(1)}, f32[1024]{0:T(1024)}, u32[]{:S(2)}) copy-start(f32[1024]{0:T(1024)} %param.21) | copy-start | bytes 12292
  167.0 59.1 %all-to-all-start.2 = ((bf16[8,256,1024]{1,2,0:T(8,128)(2,1)}), bf16[8,256,1024]{1,2,0:T(8,128)(2,1)}, u32[]{:S(2)}, u32[]{:S(2)}) async-start(bf16[8,256,1024]{1,2,0:T(8,128)(2,1)} %stack.3), calls=%async_computation.2 | async-start | bytes 8388608 | tf_op jit(solution)/shard_map/all_to_all | solution.py:95
  226.1 32.4 %copy-start.4 = (bf16[256,1024]{1,0:T(8,128)(2,1)S(1)}, bf16[256,1024]{1,0:T(8,128)(2,1)}, u32[]{:S(2)}) copy-start(bf16[256,1024]{1,0:T(8,128)(2,1)} %param.23) | copy-start | bytes 1572868
  238.0 21.8 %copy-start.2 = (bf16[256,1024]{1,0:T(8,128)(2,1)}, bf16[256,1024]{1,0:T(8,128)(2,1)S(1)}, u32[]{:S(2)}) copy-start(bf16[256,1024]{1,0:T(8,128)(2,1)S(1)} %get-tuple-element.100) | copy-start | bytes 1572868
Sparse Core Ops, SparseCore 0:
  9.7 102.6 all-gather.1
